TPU v7x, 32 devices: a whole 2x2x4 slice. The times are simulated.
32 devices in a mesh: dom: 8 (over z, y), case: 4 (over x, core).
Axes of the slice: x: 2, y: 2, z: 4, core: 2. Of those that a mesh axis runs over, the one named last changes fastest.
Arguments:
- dual_ops: float32 [16, 1536, 1536], P('dom')
- modes: bfloat16 [16, 16, 1536], P('dom'), may hold values from -0.15625 to 0.15625
- coarse_rows: float32 [16, 8, 16, 16], P('dom'), may hold values from -1 to 1
- coarse_cols: int32 [16, 8], P('dom'), may hold values from 0 to 15, as said below
- row_perm: int32 [16, 1536], P('dom'), may hold values from 0 to 1535, each once within a row
- iface_size: int32 [16], P('dom'), may hold values from 256 to 768, as said below
- rhs: float32 [16, 768, 512], P('dom', None, 'case'), may hold values from -6 to 6
Outputs:
- solution: float32 [16, 768, 512], P('dom', None, 'case')
- residual: float32 [16, 768, 512], P('dom', None, 'case')
- history: float32 [4, 512], P(None, 'case')
- peak_norm: float32 [4], replicated
Inputs may be any that keep to these rules, and one draw needn't show every extreme that they name: `iface_size`: interfaces carry between 256 and 768 multipliers; both ends are reached in every draw. `coarse_cols`: for every subdomain s the first three entries are s, (s - 1) mod 16 and (s + 1) mod 16; the others are any subdomains, repeats allowed. `row_perm`: each row is a permutation of the local rows.
All inputs are finite; a program needn't handle non-finite values.
Results may differ from a plain program's by a relative error of at most 0.0056.
Values may be sent and summed in bfloat16 or wider, within the bound.
A program may use at most 192 MiB of HBM per device.

v0:
```python
import jax
import jax.numpy as jnp
from jax import lax
from jax.sharding import PartitionSpec as P

STEPS = 4
low_bound = 2.0
high_bound = 14.0
epsilon = 1e-06
highest = lax.Precision.HIGHEST


def from_behind(block, axis, distance):
    devices = range(lax.axis_size(axis))
    route = [((i - distance) % len(devices), i) for i in devices]
    return lax.ppermute(block, axis, route)


def slot_form(left_side, right_side):
    return jnp.concatenate([-left_side, right_side], axis=1)


def shards(dual_ops, modes, coarse_rows, coarse_cols, row_perm, iface_size, rhs):
    sub_count, half_width, case_count = rhs.shape
    dom_count = lax.axis_size("dom") * sub_count
    live_mask = (
        lax.broadcasted_iota(jnp.int32, (sub_count, half_width), 1) < iface_size[:, None]
    ).astype(jnp.float32)[:, :, None]
    slot_ops = jax.vmap(lambda matrix, ordering: matrix[ordering].T[ordering])(dual_ops, row_perm)
    slot_modes_low = jax.vmap(lambda block_rows, ordering: block_rows[:, ordering])(modes, row_perm)
    slot_modes = slot_modes_low.astype(jnp.float32)
    int_pack = jnp.concatenate([coarse_cols, iface_size[:, None]], axis=1)
    prior_ints = from_behind(int_pack[-1], "dom", 1)
    next_ints = from_behind(int_pack[0], "dom", -1)
    prior_modes = from_behind(slot_modes_low[-1], "dom", 1)
    next_modes = from_behind(slot_modes_low[0], "dom", -1)
    prior_blocks = from_behind(coarse_rows[-1], "dom", 1)
    next_blocks = from_behind(coarse_rows[0], "dom", -1)
    ext_ints = jnp.concatenate([prior_ints[None], int_pack, next_ints[None]], axis=0)
    block_count = coarse_cols.shape[1]
    ext_cols = ext_ints[:, :block_count]
    ext_size = ext_ints[:, block_count]
    ext_modes = jnp.concatenate(
        [prior_modes[None], slot_modes_low, next_modes[None]], axis=0
    ).astype(jnp.float32)
    ext_blocks = jnp.concatenate([prior_blocks[None], coarse_rows, next_blocks[None]], axis=0)
    ext_live = (
        lax.broadcasted_iota(jnp.int32, (sub_count + 2, half_width), 1) < ext_size[:, None]
    ).astype(jnp.float32)[:, :, None]

    def build_local(vector):
        prior_rim = from_behind(vector[-1], "dom", 1)
        left_side = jnp.concatenate([prior_rim[None], vector[:-1]], axis=0)
        return slot_form(left_side, vector)

    def select_columns(columns, all_coefficients):
        table = (
            columns[:, :, None] == lax.broadcasted_iota(jnp.int32, (1, 1, dom_count), 2)
        ).astype(jnp.float32)
        return jnp.einsum(
            "sqd,djc->sqjc", table, all_coefficients.astype(jnp.float32), precision=highest
        )

    def gather_coefficients(slot_rows):
        coefficients = jnp.einsum("sjn,snc->sjc", slot_modes, slot_rows, precision=highest).astype(
            jnp.bfloat16
        )
        return lax.all_gather(coefficients, "dom", axis=0, tiled=True)

    centre = 0.5 * (high_bound + low_bound)
    radius = 0.5 * (high_bound - low_bound)
    spread_ratio = centre / radius
    ratio_now = 1.0 / spread_ratio
    start_vector = rhs * live_mask
    picked = select_columns(coarse_cols, gather_coefficients(build_local(start_vector)))
    amounts = jnp.einsum("sqij,sqjc->sic", coarse_rows, picked, precision=highest)
    slot_rows = jnp.einsum("sjn,sjc->snc", slot_modes, amounts, precision=highest)
    lower_half = slot_rows[:, :half_width]
    upper_half = slot_rows[:, half_width:]
    later_rim = from_behind(lower_half[0], "dom", -1)
    following = jnp.concatenate([lower_half[1:], later_rim[None]], axis=0)
    residual = start_vector - (upper_half - following) * live_mask
    direction = residual / centre
    local_residual = build_local(residual)
    local_direction = local_residual / centre
    solution = jnp.zeros_like(rhs)
    norm_list = []
    for turn_index in range(STEPS):
        solution = solution + direction
        product = jnp.einsum("smn,smc->snc", slot_ops, local_direction, precision=highest)
        local_lower_half = product[:, :half_width]
        local_upper_half = product[:, half_width:]
        prior_upper = from_behind(local_upper_half[-1], "dom", 1)
        later_lower = from_behind(local_lower_half[0], "dom", -1)
        local_following = jnp.concatenate([local_lower_half[1:], later_lower[None]], axis=0)
        mapped = (local_upper_half - local_following) * live_mask
        first_value = (prior_upper - local_lower_half[0]) * ext_live[0]
        local_left_side = jnp.concatenate([first_value[None], mapped[:-1]], axis=0)
        mapped, local_mapped = (mapped, slot_form(local_left_side, mapped))
        wide_picked = select_columns(ext_cols, gather_coefficients(local_mapped))
        wide_amounts = jnp.einsum("sqij,sqjc->sic", ext_blocks, wide_picked, precision=highest)
        spread = jnp.einsum("sjn,sjc->snc", ext_modes, wide_amounts, precision=highest)
        lower_part = spread[:, :half_width]
        upper_part = spread[:, half_width:]
        joined = (upper_part[:-1] - lower_part[1:]) * ext_live[:-1]
        correction = joined[1:]
        local_correction = slot_form(joined[:-1], joined[1:])
        residual = residual - (mapped - correction)
        local_residual = local_residual - (local_mapped - local_correction)
        partial_value = jnp.sum(residual * residual, axis=(0, 1))
        norm_list.append(jnp.sqrt(lax.psum(partial_value, "dom") + epsilon))
        if turn_index + 1 < STEPS:
            ratio_next = 1.0 / (2.0 * spread_ratio - ratio_now)
            direction = ratio_next * ratio_now * direction + 2.0 * ratio_next / radius * residual
            local_direction = (
                ratio_next * ratio_now * local_direction
                + 2.0 * ratio_next / radius * local_residual
            )
            ratio_now = ratio_next
    history = jnp.stack(norm_list)
    peak_norm = lax.pmax(jnp.max(history, axis=1), "case")
    return (solution, residual, history, peak_norm)


def solution(mesh):
    in_specs = (
        P("dom", None, None),
        P("dom", None, None),
        P("dom", None, None, None),
        P("dom", None),
        P("dom", None),
        P("dom"),
        P("dom", None, "case"),
    )
    out_specs = (P("dom", None, "case"), P("dom", None, "case"), P(None, "case"), P())
    return jax.shard_map(shards, mesh=mesh, in_specs=in_specs, out_specs=out_specs, check_vma=False)
```

profile of v0, /device:TPU:0, one launch (start us, length us, event | category | flops | bytes accessed | tf_op | source)
XLA Modules:
  0.0 592.4 jit_solution(7699816429259120163)
XLA Ops:
  1.4 1.4 broadcast_multiply_fusion
  3.6 3.0 collective-permute-start
  7.3 16.5 %gather_fusion = bf16[3072,16]{1,0:T(8,128)(2,1)S(1)} fusion(bf16[2,16,1536]{1,2,0:T(8,128)(2,1)S(1)} %copy.28, s32[3072]{0:T(1024)S(1)} %reshape.35), kind=kCustom, calls=%fused_computation | custom fusion | bytes 221184 | tf_op jit(solution)/shard_map/vmap()/gather | solution.py:30
  23.9 0.9 fusion.33
  24.8 30.9 %all_gather.15 = bf16[16,16,128]{2,1,0:T(8,128)(2,1)S(1)} all-gather(bf16[2,16,128]{2,1,0:T(8,128)(2,1)S(1)} %fusion.33), channel_id=1, replica_groups=mesh['dom'=8,'case'=4] {'dom'}, dimensions={0}, use_global_device_ids=true | all-gather | bytes 73728 | tf_op jit(solution)/shard_map/all_gather | solution.py:68
  57.9 2.7 collective-permute-start.1
  60.6 2.0 collective-permute-start.8
  63.2 2.7 collective-permute-start.7
  66.2 68.1 %gather_fusion.1 = f32[3072,1536]{1,0:T(8,128)} fusion(f32[2,1536,1536]{2,1,0:T(8,128)} %param.7, s32[3072]{0:T(1024)S(1)} %reshape.35), kind=kCustom, calls=%fused_computation.1 | custom fusion | bytes 37773312 | tf_op jit(solution)/shard_map/vmap()/gather | solution.py:29
  134.3 18.7 %copy.34 = f32[2,1536,1536]{1,2,0:T(8,128)} copy(f32[2,1536,1536]{2,1,0:T(8,128)} %bitcast.153) | data formatting | bytes 37748736 | tf_op jit(solution)/shard_map/vmap()/gather | solution.py:29
  153.0 68.1 %gather_fusion.2 = f32[3072,1536]{1,0:T(8,128)} fusion(f32[2,1536,1536]{2,1,0:T(8,128)} %bitcast.146, s32[3072]{0:T(1024)S(1)} %reshape.35), kind=kCustom, calls=%fused_computation.2 | custom fusion | bytes 37773312 | tf_op jit(solution)/shard_map/vmap()/gather | solution.py:29
  221.8 1.7 fusion.44
  224.0 4.5 collective-permute-start.5
  228.6 5.4 collective-permute-done.2
  234.1 32.9 %fusion.18 = f32[2,1536,128]{2,1,0:T(8,128)S(1)} fusion(f32[2,1536,1536]{2,1,0:T(8,128)} %bitcast.147, f32[2,768,128]{2,1,0:T(8,128)S(1)} %fusion.44, f32[2,768,128]{2,1,0:T(8,128)S(1)} %maximum_negate_fusion.1), kind=kOutput, calls=%fused_computation.29 | convolution fusion | flops 7248543744 | bytes 22020096 | tf_op jit(solution)/shard_map/smn,smc->snc/dot_general | solution.py:90
  267.1 2.6 collective-permute-start.3
  270.1 5.5 collective-permute-done.3
  275.9 4.6 collective-permute-done.10
  281.7 30.7 %all_gather.16 = bf16[16,16,128]{2,1,0:T(8,128)(2,1)S(1)} all-gather(bf16[2,16,128]{2,1,0:T(8,128)(2,1)S(1)} %fusion.27), channel_id=1, replica_groups=mesh['dom'=8,'case'=4] {'dom'}, dimensions={0}, use_global_device_ids=true | all-gather | bytes 73728 | tf_op jit(solution)/shard_map/all_gather | solution.py:68
  313.3 1.6 fusion.109
  315.3 1.3 multiply_reduce_fusion.3
  317.5 31.7 %fusion.115 = f32[2,1536,128]{2,1,0:T(8,128)S(1)} fusion(f32[2,1536,1536]{2,1,0:T(8,128)S(1)} %bitcast.150, f32[2,1536,128]{2,1,0:T(8,128)S(1)} %multiply_add_fusion.1), kind=kOutput, calls=%fused_computation.185 | convolution fusion | flops 7247757312 | bytes 22020096 | tf_op jit(solution)/shard_map/smn,smc->snc/dot_general | solution.py:90
  349.3 1.6 collective-permute-start.11
  351.3 5.8 collective-permute-done.11
  357.6 3.9 collective-permute-done.12
  362.7 30.5 %all_gather.17 = bf16[16,16,128]{2,1,0:T(8,128)(2,1)S(1)} all-gather(bf16[2,16,128]{2,1,0:T(8,128)(2,1)S(1)} %fusion.28), channel_id=1, replica_groups=mesh['dom'=8,'case'=4] {'dom'}, dimensions={0}, use_global_device_ids=true | all-gather | bytes 73728 | tf_op jit(solution)/shard_map/all_gather | solution.py:68
  394.1 1.6 fusion.108
  396.8 1.3 multiply_reduce_fusion.2
  398.1 1.6 fusion.5
  399.7 33.1 %fusion.20 = f32[2,1536,128]{2,1,0:T(8,128)} fusion(f32[2,1536,1536]{2,1,0:T(8,128)S(1)} %bitcast.151, f32[2,1536,128]{2,1,0:T(8,128)} %fusion.5, f32[2,1536,128]{2,1,0:T(8,128)S(1)} %multiply_add_fusion.1), kind=kOutput, calls=%fused_computation.31 | convolution fusion | flops 7248936960 | bytes 23592960 | tf_op jit(solution)/shard_map/smn,smc->snc/dot_general | solution.py:90
  432.8 1.4 slice_bitcast_fusion.2
  434.3 2.1 collective-permute-start.13
  436.3 5.8 collective-permute-done.13
  442.6 4.3 collective-permute-done.14
  448.1 30.5 %all_gather.18 = bf16[16,16,128]{2,1,0:T(8,128)(2,1)S(1)} all-gather(bf16[2,16,128]{2,1,0:T(8,128)(2,1)S(1)} %fusion.29), channel_id=1, replica_groups=mesh['dom'=8,'case'=4] {'dom'}, dimensions={0}, use_global_device_ids=true | all-gather | bytes 73728 | tf_op jit(solution)/shard_map/all_gather | solution.py:68
  479.5 1.6 fusion.107
  482.3 1.7 multiply_reduce_fusion.1
  484.1 32.5 %fusion.9 = f32[2,1536,128]{2,1,0:T(8,128)S(1)} fusion(f32[2,1536,1536]{2,1,0:T(8,128)S(1)} %bitcast.152, f32[2,1536,128]{2,1,0:T(8,128)S(1)} %copy-done, f32[2,768,128]{2,1,0:T(8,128)} %get-tuple-element.35, f32[2,768,128]{2,1,0:T(8,128)} %get-tuple-element.34, f32[2,1536,128]{2,1,0:T(8,128)S(1)} %multiply_add_fusion.1, f32[2,768,128]{2,1,0:T(8,128)S(1)} %fusion.40, ...), kind=kOutput, calls=%fused_computation.19 | convolution fusion | flops 7251689472 | bytes 26738688 | tf_op jit(solution)/shard_map/smn,smc->snc/dot_general | solution.py:90
  516.7 1.8 collective-permute-start.15
  518.8 5.8 collective-permute-done.15
  525.0 4.0 collective-permute-done.16
  529.3 0.9 fusion.30
  530.2 30.5 %all_gather.19 = bf16[16,16,128]{2,1,0:T(8,128)(2,1)S(1)} all-gather(bf16[2,16,128]{2,1,0:T(8,128)(2,1)S(1)} %fusion.30), channel_id=1, replica_groups=mesh['dom'=8,'case'=4] {'dom'}, dimensions={0}, use_global_device_ids=true | all-gather | bytes 73728 | tf_op jit(solution)/shard_map/all_gather | solution.py:68
  561.6 1.6 fusion.106
  563.4 0.9 copy-done.5
  564.6 1.7 multiply_reduce_fusion
  566.3 19.1 %all-reduce = (f32[128]{0:T(128)S(1)}, f32[128]{0:T(128)S(1)}, f32[128]{0:T(128)S(1)}, f32[128]{0:T(128)S(1)}) all-reduce(f32[128]{0:T(128)S(1)} %get-tuple-element.16, f32[128]{0:T(128)S(1)} %get-tuple-element.14, f32[128]{0:T(128)S(1)} %get-tuple-element.12, f32[128]{0:T(128)S(1)} %get-tuple-element.10), channel_id=1, replica_groups=mesh['dom'=8,'case'=4] {'dom'}, use_global_device_ids=true, to_apply=%region_7.0 | all-reduce | flops 512 | bytes 4096 | tf_op jit(solution)/shard_map/psum | solution.py:111
  586.0 6.2 %pmax.7 = f32[4]{0:T(128)} all-reduce(f32[4]{0:T(128)S(1)} %get-tuple-element.8), channel_id=1, replica_groups=mesh['dom'=8,'case'=4] {'case'}, use_global_device_ids=true, to_apply=%region_9.0 | all-reduce | flops 4 | bytes 32 | tf_op jit(solution)/shard_map/pmax | solution.py:121
  (118 shorter events, 21.8 us)
Async XLA Ops:
  1.4 5.3 copy-start.11
  2.8 4.2 copy-start.12
  2.8 4.3 copy-start.8
  2.8 4.4 copy-start.14
  3.6 20.2 %collective-permute-start = (f32[768,128]{1,0:T(8,128)}, f32[768,128]{1,0:T(8,128)S(1)}, u32[]{:S(2)}, u32[]{:S(2)}) collective-permute-start(f32[768,128]{1,0:T(8,128)} %get-tuple-element.43), channel_id=1, source_target_pairs={{28,0},{0,4},{4,8},{8,12},{12,16},{16,20},{20,24},{24,28},{29,1},{... | collective-permute-start | bytes 1179656 | tf_op jit(solution)/shard_map/ppermute | solution.py:16
  7.0 16.8 %copy-start.13 = (s32[2,8]{1,0:T(2,128)S(1)}, s32[2,8]{1,0:T(2,128)}, u32[]{:S(2)}) copy-start(s32[2,8]{1,0:T(2,128)} %param.10) | copy-start | bytes 196
  57.9 163.1 %collective-permute-start.1 = (f32[768,128]{1,0:T(8,128)S(1)}, f32[768,128]{1,0:T(8,128)S(1)}, u32[]{:S(2)}, u32[]{:S(2)}) collective-permute-start(f32[768,128]{1,0:T(8,128)S(1)} %get-tuple-element.33), channel_id=1, source_target_pairs={{4,0},{8,4},{12,8},{16,12},{20,16},{24,20},{28,24},{0,28},{5,1},{9... | collective-permute-start | bytes 1179656 | tf_op jit(solution)/shard_map/ppermute | solution.py:16
  60.6 163.5 %collective-permute-start.9 = (s32[9]{0:T(128)S(1)}, s32[9]{0:T(128)S(1)}, u32[]{:S(2)}, u32[]{:S(2)}) collective-permute-start(s32[9]{0:T(128)S(1)} %get-tuple-element.50), channel_id=1, source_target_pairs={{4,0},{8,4},{12,8},{16,12},{20,16},{24,20},{28,24},{0,28},{5,1},{9... | collective-permute-start | bytes 116 | tf_op jit(solution)/shard_map/ppermute | solution.py:16
  60.6 168.0 %collective-permute-start.8 = (s32[9]{0:T(128)S(1)}, s32[9]{0:T(128)S(1)}, u32[]{:S(2)}, u32[]{:S(2)}) collective-permute-start(s32[9]{0:T(128)S(1)} %get-tuple-element.49), channel_id=1, source_target_pairs={{28,0},{0,4},{4,8},{8,12},{12,16},{16,20},{20,24},{24,28},{29,1},{... | collective-permute-start | bytes 116 | tf_op jit(solution)/shard_map/ppermute | solution.py:16
  63.2 249.4 %collective-permute-start.7 = (f32[8,16,16]{2,1,0:T(8,128)}, f32[8,16,16]{2,1,0:T(8,128)S(1)}, u32[]{:S(2)}, u32[]{:S(2)}) collective-permute-start(f32[8,16,16]{2,1,0:T(8,128)} %get-tuple-element.46), channel_id=1, source_target_pairs={{4,0},{8,4},{12,8},{16,12},{20,16},{24,20},{28,24},{0,28},{5,1},{9... | collective-permute-start | bytes 24584 | tf_op jit(solution)/shard_map/ppermute | solution.py:16
  66.0 246.7 %collective-permute-start.6 = (f32[8,16,16]{2,1,0:T(8,128)}, f32[8,16,16]{2,1,0:T(8,128)S(1)}, u32[]{:S(2)}, u32[]{:S(2)}) collective-permute-start(f32[8,16,16]{2,1,0:T(8,128)} %get-tuple-element.45), channel_id=1, source_target_pairs={{28,0},{0,4},{4,8},{8,12},{12,16},{16,20},{20,24},{24,28},{29,1},{... | collective-permute-start | bytes 24584 | tf_op jit(solution)/shard_map/ppermute | solution.py:16
  221.0 0.7 copy-start.10
  223.5 10.6 %collective-permute-start.2 = (f32[768,128]{1,0:T(8,128)S(1)}, f32[768,128]{1,0:T(8,128)S(1)}, u32[]{:S(2)}, u32[]{:S(2)}) collective-permute-start(f32[768,128]{1,0:T(8,128)S(1)} %get-tuple-element.41), channel_id=1, source_target_pairs={{28,0},{0,4},{4,8},{8,12},{12,16},{16,20},{20,24},{24,28},{29,1},{... | collective-permute-start | bytes 1179656 | tf_op jit(solution)/shard_map/ppermute | solution.py:16
  224.0 89.3 %collective-permute-start.5 = (bf16[16,1536]{1,0:T(8,128)(2,1)S(1)}, bf16[16,1536]{1,0:T(8,128)(2,1)S(1)}, u32[]{:S(2)}, u32[]{:S(2)}) collective-permute-start(bf16[16,1536]{1,0:T(8,128)(2,1)S(1)} %get-tuple-element.48), channel_id=1, source_target_pairs={{4,0},{8,4},{12,8},{16,12},{20,16},{24,20},{28,24},{0,28},{5,1},{9... | collective-permute-start | bytes 147464 | tf_op jit(solution)/shard_map/ppermute | solution.py:16
  234.1 83.4 %slice-start = ((s8[18874368]{0:T(1024)(128)(4,1)}), s8[4194304]{0:T(1024)(128)(4,1)S(1)}, s32[]{:S(2)}) async-start(s8[18874368]{0:T(1024)(128)(4,1)} %bitcast.148), calls=%async_computation | async-start | bytes 8388608
  234.1 83.4 %slice-start.1 = ((s8[18874368]{0:T(1024)(128)(4,1)}), s8[4194304]{0:T(1024)(128)(4,1)S(1)}, s32[]{:S(2)}) async-start(s8[18874368]{0:T(1024)(128)(4,1)} %bitcast.148), calls=%async_computation.1 | async-start | bytes 8388608
  234.1 83.4 %slice-start.2 = ((s8[18874368]{0:T(1024)(128)(4,1)}), s8[4194304]{0:T(1024)(128)(4,1)S(1)}, s32[]{:S(2)}) async-start(s8[18874368]{0:T(1024)(128)(4,1)} %bitcast.148), calls=%async_computation.2 | async-start | bytes 8388608
  267.1 8.4 %collective-permute-start.3 = (f32[768,128]{1,0:T(8,128)S(1)}, f32[768,128]{1,0:T(8,128)S(1)}, u32[]{:S(2)}, u32[]{:S(2)}) collective-permute-start(f32[768,128]{1,0:T(8,128)S(1)} %get-tuple-element.30), channel_id=1, source_target_pairs={{4,0},{8,4},{12,8},{16,12},{20,16},{24,20},{28,24},{0,28},{5,1},{9... | collective-permute-start | bytes 1179656 | tf_op jit(solution)/shard_map/ppermute | solution.py:16
  269.9 10.6 %collective-permute-start.10 = (f32[768,128]{1,0:T(8,128)S(1)}, f32[768,128]{1,0:T(8,128)S(1)}, u32[]{:S(2)}, u32[]{:S(2)}) collective-permute-start(f32[768,128]{1,0:T(8,128)S(1)} %get-tuple-element.29), channel_id=1, source_target_pairs={{28,0},{0,4},{4,8},{8,12},{12,16},{16,20},{20,24},{24,28},{29,1},{... | collective-permute-start | bytes 1179656 | tf_op jit(solution)/shard_map/ppermute | solution.py:16
  275.5 37.8 %collective-permute-start.4 = (bf16[16,1536]{1,0:T(8,128)(2,1)S(1)}, bf16[16,1536]{1,0:T(8,128)(2,1)S(1)}, u32[]{:S(2)}, u32[]{:S(2)}) collective-permute-start(bf16[16,1536]{1,0:T(8,128)(2,1)S(1)} %get-tuple-element.47), channel_id=1, source_target_pairs={{28,0},{0,4},{4,8},{8,12},{12,16},{16,20},{20,24},{24,28},{29,1},{... | collective-permute-start | bytes 147464 | tf_op jit(solution)/shard_map/ppermute | solution.py:16
  280.8 36.7 %slice-start.3 = ((s8[18874368]{0:T(1024)(128)(4,1)}), s8[4194304]{0:T(1024)(128)(4,1)S(1)}, s32[]{:S(2)}) async-start(s8[18874368]{0:T(1024)(128)(4,1)} %bitcast.148), calls=%async_computation.3 | async-start | bytes 8388608
  315.3 2.2 slice-start.4
  316.6 0.9 copy-start.2
  349.3 7.9 %collective-permute-start.11 = (f32[768,128]{1,0:T(8,128)S(1)}, f32[768,128]{1,0:T(8,128)S(1)}, u32[]{:S(2)}, u32[]{:S(2)}) collective-permute-start(f32[768,128]{1,0:T(8,128)S(1)} %get-tuple-element.27), channel_id=1, source_target_pairs={{4,0},{8,4},{12,8},{16,12},{20,16},{24,20},{28,24},{0,28},{5,1},{9... | collective-permute-start | bytes 1179656 | tf_op jit(solution)/shard_map/ppermute | solution.py:16
  350.9 10.6 %collective-permute-start.12 = (f32[768,128]{1,0:T(8,128)S(1)}, f32[768,128]{1,0:T(8,128)S(1)}, u32[]{:S(2)}, u32[]{:S(2)}) collective-permute-start(f32[768,128]{1,0:T(8,128)S(1)} %get-tuple-element.26), channel_id=1, source_target_pairs={{28,0},{0,4},{4,8},{8,12},{12,16},{16,20},{20,24},{24,28},{29,1},{... | collective-permute-start | bytes 1179656 | tf_op jit(solution)/shard_map/ppermute | solution.py:16
  395.7 1.1 copy-start.4
  396.8 1.3 copy-start.3
  432.8 9.4 %copy-start.1 = (f32[2,1536,128]{2,1,0:T(8,128)S(1)}, f32[2,1536,128]{2,1,0:T(8,128)}, u32[]{:S(2)}) copy-start(f32[2,1536,128]{2,1,0:T(8,128)} %fusion.20) | copy-start | bytes 4718596
  434.3 7.9 %collective-permute-start.13 = (f32[768,128]{1,0:T(8,128)S(1)}, f32[768,128]{1,0:T(8,128)S(1)}, u32[]{:S(2)}, u32[]{:S(2)}) collective-permute-start(f32[768,128]{1,0:T(8,128)S(1)} %get-tuple-element.24), channel_id=1, source_target_pairs={{4,0},{8,4},{12,8},{16,12},{20,16},{24,20},{28,24},{0,28},{5,1},{9... | collective-permute-start | bytes 1179656 | tf_op jit(solution)/shard_map/ppermute | solution.py:16
  436.3 10.6 %collective-permute-start.14 = (f32[768,128]{1,0:T(8,128)S(1)}, f32[768,128]{1,0:T(8,128)S(1)}, u32[]{:S(2)}, u32[]{:S(2)}) collective-permute-start(f32[768,128]{1,0:T(8,128)S(1)} %get-tuple-element.23), channel_id=1, source_target_pairs={{28,0},{0,4},{4,8},{8,12},{12,16},{16,20},{20,24},{24,28},{29,1},{... | collective-permute-start | bytes 1179656 | tf_op jit(solution)/shard_map/ppermute | solution.py:16
  447.2 32.4 %copy-start.7 = (f32[2,768,128]{2,1,0:T(8,128)}, f32[2,768,128]{2,1,0:T(8,128)S(1)}, u32[]{:S(2)}) copy-start(f32[2,768,128]{2,1,0:T(8,128)S(1)} %maximum_negate_fusion.4) | copy-start | bytes 2359300
  481.1 1.1 copy-start.6
  482.3 1.8 copy-start
  516.7 7.9 %collective-permute-start.15 = (f32[768,128]{1,0:T(8,128)S(1)}, f32[768,128]{1,0:T(8,128)S(1)}, u32[]{:S(2)}, u32[]{:S(2)}) collective-permute-start(f32[768,128]{1,0:T(8,128)S(1)} %get-tuple-element.21), channel_id=1, source_target_pairs={{4,0},{8,4},{12,8},{16,12},{20,16},{24,20},{28,24},{0,28},{5,1},{9... | collective-permute-start | bytes 1179656 | tf_op jit(solution)/shard_map/ppermute | solution.py:16
  518.5 10.5 %collective-permute-start.16 = (f32[768,128]{1,0:T(8,128)S(1)}, f32[768,128]{1,0:T(8,128)S(1)}, u32[]{:S(2)}, u32[]{:S(2)}) collective-permute-start(f32[768,128]{1,0:T(8,128)S(1)} %get-tuple-element.20), channel_id=1, source_target_pairs={{28,0},{0,4},{4,8},{8,12},{12,16},{16,20},{20,24},{24,28},{29,1},{... | collective-permute-start | bytes 1179656 | tf_op jit(solution)/shard_map/ppermute | solution.py:16
  563.2 1.1 copy-start.5
  563.2 1.4 copy-start.9
where the time goes:
time: 601 us; the launch traced here: 592 us
  local copies, waits for them, and re-layouts  181 us (30%)
  blocking collectives  178 us (30%)
  matrix products  146 us (24%)
  waiting for transfers between devices  45.1 us (8%)
  starting transfers between devices  24.3 us (4%)
  other arithmetic  16.3 us (3%)
    gather x3, local copies, waits for them, and re-layouts, shards(): matrix[ordering].T[ordering]  155 us
    all_gather x5, blocking collectives, gather_coefficients(): return lax.all_gather(coefficients, 'dom', axis=0, tiled=True)  153 us
    dot_general x4, matrix products, shards(): jnp.einsum('smn,smc->snc', slot_ops, local_direction, precision=highest)  130 us
    ppermute x17, waiting for transfers between devices, from_behind(): return lax.ppermute(block, axis, route)  45.1 us
    ppermute x17, starting transfers between devices, from_behind(): return lax.ppermute(block, axis, route)  24.3 us
    psum x1, blocking collectives, shards(): norm_list.append(jnp.sqrt(lax.psum(partial_value, 'dom') + epsilon))  19.1 us
    gather x3, local copies, waits for them, and re-layouts, shards(): block_rows[:, ordering]  16.7 us
  transfers between devices with their start and end apart: 17, of which 9 were waited for; matrix products, arithmetic and copies ran while one was open for 36% of the time, Pallas kernels for 0%

commit v1 on v0

--- a/solution.py
+++ b/solution.py
@@ -8,6 +8,18 @@
 high_bound = 14.0
 epsilon = 1e-06
 highest = lax.Precision.HIGHEST
+
+
+def collect(shard, axis, dim):
+    ways, here, lap = (lax.axis_size(axis), lax.axis_index(axis), shard.shape[dim])
+    line, have = (shard, 1)
+    while have < ways:
+        line = jnp.concatenate(
+            [line, lax.ppermute(line, axis, [(d, (d - have) % ways) for d in range(ways)])],
+            axis=dim,
+        )
+        have = 2 * have
+    return jnp.roll(line, here * lap, axis=dim)
 
 
 def from_behind(block, axis, distance):
@@ -65,7 +77,7 @@
         coefficients = jnp.einsum("sjn,snc->sjc", slot_modes, slot_rows, precision=highest).astype(
             jnp.bfloat16
         )
-        return lax.all_gather(coefficients, "dom", axis=0, tiled=True)
+        return collect(coefficients, "dom", 0)
 
     centre = 0.5 * (high_bound + low_bound)
     radius = 0.5 * (high_bound - low_bound)

time: 601 us -> 540 us (0.90)
  blocking collectives: 178 us -> 29.3 us
  waiting for transfers between devices: 45.1 us -> 95.2 us
  starting transfers between devices: 24.3 us -> 55.1 us
    all_gather x5 -> x0, blocking collectives: 153 us -> none  [gather_coefficients(): return lax.all_gather(coefficients, 'dom', axis=0, tiled=True)]
    ppermute x0 -> x15, waiting for transfers between devices: none -> 40.6 us  [collect(): lax.ppermute(line, axis, [(d, (d - have) % ways) for d in range(ways)])]
    ppermute x17, starting transfers between devices: 24.3 us -> 40.4 us  [from_behind(): return lax.ppermute(block, axis, route)]
    ppermute x0 -> x15, starting transfers between devices: none -> 14.8 us  [collect(): lax.ppermute(line, axis, [(d, (d - have) % ways) for d in range(ways)])]
    ppermute x17, waiting for transfers between devices: 45.1 us -> 54.6 us  [from_behind(): return lax.ppermute(block, axis, route)]
  transfers between devices with their start and end apart: 17 -> 32, of which waited for: 9 -> 20; matrix products, arithmetic and copies ran while one was open for 36% -> 33% of each run, Pallas kernels for 0% -> 0%
where the time goes in v1:
time: 540 us; the launch traced here: 531 us
  local copies, waits for them, and re-layouts  183 us (34%)
  matrix products  147 us (27%)
  waiting for transfers between devices  95.2 us (18%)
  starting transfers between devices  55.1 us (10%)
  blocking collectives  29.3 us (5%)
  other arithmetic  19.4 us (4%)
    gather x3, local copies, waits for them, and re-layouts, shards(): matrix[ordering].T[ordering]  155 us
    dot_general x4, matrix products, shards(): jnp.einsum('smn,smc->snc', slot_ops, local_direction, precision=highest)  132 us
    ppermute x17, waiting for transfers between devices, from_behind(): return lax.ppermute(block, axis, route)  54.6 us
    ppermute x15, waiting for transfers between devices, collect(): lax.ppermute(line, axis, [(d, (d - have) % ways) for d in range(ways)])  40.6 us
    ppermute x17, starting transfers between devices, from_behind(): return lax.ppermute(block, axis, route)  40.4 us
    psum x1, blocking collectives, shards(): norm_list.append(jnp.sqrt(lax.psum(partial_value, 'dom') + epsilon))  23.1 us
    gather x3, local copies, waits for them, and re-layouts, shards(): block_rows[:, ordering]  16.7 us
    ppermute x15, starting transfers between devices, collect(): lax.ppermute(line, axis, [(d, (d - have) % ways) for d in range(ways)])  14.8 us
  transfers between devices with their start and end apart: 32, of which 20 were waited for; matrix products, arithmetic and copies ran while one was open for 33% of the time, Pallas kernels for 0%

profile of v1, /device:TPU:0, one launch (start us, length us, event | category | flops | bytes accessed | tf_op | source)
XLA Modules:
  0.0 531.2 jit_solution(16824667205969705844)
XLA Ops:
  3.6 3.0 collective-permute-start
  7.0 16.5 %gather_fusion = bf16[3072,16]{1,0:T(8,128)(2,1)S(1)} fusion(bf16[2,16,1536]{1,2,0:T(8,128)(2,1)S(1)} %copy.18, s32[3072]{0:T(1024)S(1)} %reshape.35), kind=kCustom, calls=%fused_computation | custom fusion | bytes 221184 | tf_op jit(solution)/shard_map/vmap()/gather | solution.py:42
  24.5 3.1 collective-permute-start.1
  29.0 2.8 collective-permute-start.2
  34.7 3.4 collective-permute-done.3
  40.6 6.2 %collective-permute-start.4 = (f32[768,128]{1,0:T(8,128)S(1)}, f32[768,128]{1,0:T(8,128)S(1)}, u32[]{:S(2)}, u32[]{:S(2)}) collective-permute-start(f32[768,128]{1,0:T(8,128)S(1)} %get-tuple-element.34), channel_id=1, source_target_pairs={{4,0},{8,4},{12,8},{16,12},{20,16},{24,20},{28,24},{0,28},{5,1},{9... | collective-permute-start | bytes 1179656 | tf_op jit(solution)/shard_map/ppermute | solution.py:28
  46.9 5.2 collective-permute-done.4
  52.9 1.7 fusion.44
  54.8 5.2 collective-permute-start.12
  59.9 68.0 %gather_fusion.1 = f32[3072,1536]{1,0:T(8,128)} fusion(f32[2,1536,1536]{2,1,0:T(8,128)} %param.9, s32[3072]{0:T(1024)S(1)} %reshape.35), kind=kCustom, calls=%fused_computation.1 | custom fusion | bytes 37773312 | tf_op jit(solution)/shard_map/vmap()/gather | solution.py:41
  128.0 18.7 %copy.22 = f32[2,1536,1536]{1,2,0:T(8,128)} copy(f32[2,1536,1536]{2,1,0:T(8,128)} %bitcast.148) | data formatting | bytes 37748736 | tf_op jit(solution)/shard_map/vmap()/gather | solution.py:41
  146.7 68.0 %gather_fusion.2 = f32[3072,1536]{1,0:T(8,128)} fusion(f32[2,1536,1536]{2,1,0:T(8,128)} %bitcast.141, s32[3072]{0:T(1024)S(1)} %reshape.35), kind=kCustom, calls=%fused_computation.2 | custom fusion | bytes 37773312 | tf_op jit(solution)/shard_map/vmap()/gather | solution.py:41
  214.9 33.0 %fusion.18 = f32[2,1536,128]{2,1,0:T(8,128)S(1)} fusion(f32[2,1536,1536]{2,1,0:T(8,128)} %bitcast.142, f32[2,768,128]{2,1,0:T(8,128)S(1)} %fusion.44, f32[2,768,128]{2,1,0:T(8,128)S(1)} %maximum_negate_fusion.1), kind=kOutput, calls=%fused_computation.29 | convolution fusion | flops 7248543744 | bytes 22020096 | tf_op jit(solution)/shard_map/smn,smc->snc/dot_general | solution.py:102
  248.1 4.8 collective-permute-start.6
  253.2 11.2 %collective-permute-done.6 = f32[768,128]{1,0:T(8,128)S(1)} collective-permute-done((f32[768,128]{1,0:T(8,128)S(1)}, f32[768,128]{1,0:T(8,128)S(1)}, u32[]{:S(2)}, u32[]{:S(2)}) %collective-permute-start.6) | collective-permute-done | bytes 393248 | tf_op jit(solution)/shard_map/ppermute | solution.py:28
  268.4 2.6 collective-permute-done.14
  273.7 2.4 collective-permute-start.10
  277.6 4.8 collective-permute-start.8
  284.4 4.8 collective-permute-done.7
  289.2 1.6 fusion.144
  294.4 32.9 %fusion.150 = f32[2,1536,128]{2,1,0:T(8,128)S(1)} fusion(f32[2,1536,1536]{2,1,0:T(8,128)} %bitcast.143, f32[2,1536,128]{2,1,0:T(8,128)S(1)} %multiply_add_fusion.1), kind=kOutput, calls=%fused_computation.270 | convolution fusion | flops 7247757312 | bytes 22020096 | tf_op jit(solution)/shard_map/smn,smc->snc/dot_general | solution.py:102
  327.5 2.0 collective-permute-start.18
  329.5 12.0 %collective-permute-done.17 = f32[768,128]{1,0:T(8,128)S(1)} collective-permute-done((f32[768,128]{1,0:T(8,128)S(1)}, f32[768,128]{1,0:T(8,128)S(1)}, u32[]{:S(2)}, u32[]{:S(2)}) %collective-permute-start.17) | collective-permute-done | bytes 393248 | tf_op jit(solution)/shard_map/ppermute | solution.py:28
  343.8 3.0 collective-permute-done.19
  347.0 3.7 collective-permute-done.20
  350.7 4.8 collective-permute-done.21
  356.8 1.6 fusion.143
  360.1 1.5 fusion.5
  361.7 33.0 %fusion.20 = f32[2,1536,128]{2,1,0:T(8,128)} fusion(f32[2,1536,1536]{2,1,0:T(8,128)S(1)} %bitcast.146, f32[2,1536,128]{2,1,0:T(8,128)} %fusion.5, f32[2,1536,128]{2,1,0:T(8,128)S(1)} %multiply_add_fusion.1), kind=kOutput, calls=%fused_computation.31 | convolution fusion | flops 7248936960 | bytes 23592960 | tf_op jit(solution)/shard_map/smn,smc->snc/dot_general | solution.py:102
  396.1 5.2 collective-permute-start.22
  401.3 11.1 %collective-permute-done.22 = f32[768,128]{1,0:T(8,128)S(1)} collective-permute-done((f32[768,128]{1,0:T(8,128)S(1)}, f32[768,128]{1,0:T(8,128)S(1)}, u32[]{:S(2)}, u32[]{:S(2)}) %collective-permute-start.22) | collective-permute-done | bytes 393248 | tf_op jit(solution)/shard_map/ppermute | solution.py:28
  415.6 2.2 collective-permute-done.24
  418.4 3.1 collective-permute-done.25
  421.5 4.8 collective-permute-done.26
  427.6 1.6 fusion.142
  430.3 1.7 multiply_reduce_fusion.1
  432.1 32.7 %fusion.9 = f32[2,1536,128]{2,1,0:T(8,128)S(1)} fusion(f32[2,1536,1536]{2,1,0:T(8,128)S(1)} %bitcast.147, f32[2,1536,128]{2,1,0:T(8,128)S(1)} %copy-done.2, f32[2,768,128]{2,1,0:T(8,128)} %get-tuple-element.36, f32[2,768,128]{2,1,0:T(8,128)} %get-tuple-element.35, f32[2,1536,128]{2,1,0:T(8,128)S(1)} %multiply_add_fusion.1, f32[2,768,128]{2,1,0:T(8,128)S(1)} %fusion.40, ...), kind=kOutput, calls=%fused_computation.19 | convolution fusion | flops 7251689472 | bytes 26738688 | tf_op jit(solution)/shard_map/smn,smc->snc/dot_general | solution.py:102
  464.9 6.0 %collective-permute-start.27 = (f32[768,128]{1,0:T(8,128)S(1)}, f32[768,128]{1,0:T(8,128)S(1)}, u32[]{:S(2)}, u32[]{:S(2)}) collective-permute-start(f32[768,128]{1,0:T(8,128)S(1)} %get-tuple-element.22), channel_id=1, source_target_pairs={{4,0},{8,4},{12,8},{16,12},{20,16},{24,20},{28,24},{0,28},{5,1},{9... | collective-permute-start | bytes 1179656 | tf_op jit(solution)/shard_map/ppermute | solution.py:28
  471.0 5.4 %collective-permute-done.27 = f32[768,128]{1,0:T(8,128)S(1)} collective-permute-done((f32[768,128]{1,0:T(8,128)S(1)}, f32[768,128]{1,0:T(8,128)S(1)}, u32[]{:S(2)}, u32[]{:S(2)}) %collective-permute-start.27) | collective-permute-done | bytes 393248 | tf_op jit(solution)/shard_map/ppermute | solution.py:28
  476.8 4.8 collective-permute-done.28
  482.8 1.6 collective-permute-start.29
  484.3 2.1 collective-permute-done.29
  486.9 3.3 collective-permute-done.30
  490.2 4.8 collective-permute-done.31
  496.3 1.6 fusion.141
  499.3 1.7 multiply_reduce_fusion
  500.9 23.1 %all-reduce = (f32[128]{0:T(128)S(1)}, f32[128]{0:T(128)S(1)}, f32[128]{0:T(128)S(1)}, f32[128]{0:T(128)S(1)}) all-reduce(f32[128]{0:T(128)S(1)} %get-tuple-element.17, f32[128]{0:T(128)S(1)} %get-tuple-element.15, f32[128]{0:T(128)S(1)} %get-tuple-element.13, f32[128]{0:T(128)S(1)} %get-tuple-element.11), channel_id=1, replica_groups=mesh['dom'=8,'case'=4] {'dom'}, use_global_device_ids=true, to_apply=%region_7.9 | all-reduce | flops 512 | bytes 4096 | tf_op jit(solution)/shard_map/psum | solution.py:123
  524.8 6.2 %pmax.7 = f32[4]{0:T(128)} all-reduce(f32[4]{0:T(128)S(1)} %get-tuple-element.9), channel_id=1, replica_groups=mesh['dom'=8,'case'=4] {'case'}, use_global_device_ids=true, to_apply=%region_9.11 | all-reduce | flops 4 | bytes 32 | tf_op jit(solution)/shard_map/pmax | solution.py:133
  (178 shorter events, 44.9 us)
Async XLA Ops:
  1.4 5.2 copy-start.21
  2.8 4.2 copy-start.22
  3.6 19.9 %collective-permute-start = (f32[768,128]{1,0:T(8,128)}, f32[768,128]{1,0:T(8,128)S(1)}, u32[]{:S(2)}, u32[]{:S(2)}) collective-permute-start(f32[768,128]{1,0:T(8,128)} %get-tuple-element.44), channel_id=1, source_target_pairs={{28,0},{0,4},{4,8},{8,12},{12,16},{16,20},{20,24},{24,28},{29,1},{... | collective-permute-start | bytes 1179656 | tf_op jit(solution)/shard_map/ppermute | solution.py:28
  23.6 11.0 %copy-start.14 = (f32[2,8,16,16]{3,2,1,0:T(8,128)S(1)}, f32[2,8,16,16]{3,2,1,0:T(8,128)}, u32[]{:S(2)}) copy-start(f32[2,8,16,16]{3,2,1,0:T(8,128)} %param.11) | copy-start | bytes 49156
  23.6 14.9 %copy-start.23 = (s32[2,8]{1,0:T(2,128)S(1)}, s32[2,8]{1,0:T(2,128)}, u32[]{:S(2)}) copy-start(s32[2,8]{1,0:T(2,128)} %param.12) | copy-start | bytes 196
  24.5 4.4 collective-permute-start.1
  29.0 4.3 collective-permute-start.2
  33.3 4.8 collective-permute-start.3
  39.0 7.8 %copy-start.24 = (s32[2]{0:T(128)S(1)}, s32[2]{0:T(128)}, u32[]{:S(2)}) copy-start(s32[2]{0:T(128)} %param.14) | copy-start | bytes 28
  40.6 11.5 %collective-permute-start.4 = (f32[768,128]{1,0:T(8,128)S(1)}, f32[768,128]{1,0:T(8,128)S(1)}, u32[]{:S(2)}, u32[]{:S(2)}) collective-permute-start(f32[768,128]{1,0:T(8,128)S(1)} %get-tuple-element.34), channel_id=1, source_target_pairs={{4,0},{8,4},{12,8},{16,12},{20,16},{24,20},{28,24},{0,28},{5,1},{9... | collective-permute-start | bytes 1179656 | tf_op jit(solution)/shard_map/ppermute | solution.py:28
  54.6 160.2 %collective-permute-start.5 = (f32[768,128]{1,0:T(8,128)S(1)}, f32[768,128]{1,0:T(8,128)S(1)}, u32[]{:S(2)}, u32[]{:S(2)}) collective-permute-start(f32[768,128]{1,0:T(8,128)S(1)} %get-tuple-element.42), channel_id=1, source_target_pairs={{28,0},{0,4},{4,8},{8,12},{12,16},{16,20},{20,24},{24,28},{29,1},{... | collective-permute-start | bytes 1179656 | tf_op jit(solution)/shard_map/ppermute | solution.py:28
  54.8 160.0 %collective-permute-start.12 = (s32[9]{0:T(128)S(1)}, s32[9]{0:T(128)S(1)}, u32[]{:S(2)}, u32[]{:S(2)}) collective-permute-start(s32[9]{0:T(128)S(1)} %get-tuple-element.51), channel_id=1, source_target_pairs={{4,0},{8,4},{12,8},{16,12},{20,16},{24,20},{28,24},{0,28},{5,1},{9... | collective-permute-start | bytes 116 | tf_op jit(solution)/shard_map/ppermute | solution.py:28
  59.9 154.8 %collective-permute-start.11 = (s32[9]{0:T(128)S(1)}, s32[9]{0:T(128)S(1)}, u32[]{:S(2)}, u32[]{:S(2)}) collective-permute-start(s32[9]{0:T(128)S(1)} %get-tuple-element.50), channel_id=1, source_target_pairs={{28,0},{0,4},{4,8},{8,12},{12,16},{16,20},{20,24},{24,28},{29,1},{... | collective-permute-start | bytes 116 | tf_op jit(solution)/shard_map/ppermute | solution.py:28
  214.9 33.1 %copy-start.4 = (f32[2,768,128]{2,1,0:T(8,128)}, f32[2,768,128]{2,1,0:T(8,128)S(1)}, u32[]{:S(2)}) copy-start(f32[2,768,128]{2,1,0:T(8,128)S(1)} %maximum_negate_fusion.1) | copy-start | bytes 2359300
  248.0 17.5 %copy-start.15 = (f32[1,768,128]{2,1,0:T(8,128)}, f32[1,768,128]{2,1,0:T(8,128)S(1)}, u32[]{:S(2)}) copy-start(f32[1,768,128]{2,1,0:T(8,128)S(1)} %get-tuple-element.32) | copy-start | bytes 1179652
  248.1 16.3 %collective-permute-start.6 = (f32[768,128]{1,0:T(8,128)S(1)}, f32[768,128]{1,0:T(8,128)S(1)}, u32[]{:S(2)}, u32[]{:S(2)}) collective-permute-start(f32[768,128]{1,0:T(8,128)S(1)} %get-tuple-element.31), channel_id=1, source_target_pairs={{4,0},{8,4},{12,8},{16,12},{20,16},{24,20},{28,24},{0,28},{5,1},{9... | collective-permute-start | bytes 1179656 | tf_op jit(solution)/shard_map/ppermute | solution.py:28
  253.0 12.6 %collective-permute-start.13 = (f32[768,128]{1,0:T(8,128)S(1)}, f32[768,128]{1,0:T(8,128)S(1)}, u32[]{:S(2)}, u32[]{:S(2)}) collective-permute-start(f32[768,128]{1,0:T(8,128)S(1)} %get-tuple-element.30), channel_id=1, source_target_pairs={{28,0},{0,4},{4,8},{8,12},{12,16},{16,20},{20,24},{24,28},{29,1},{... | collective-permute-start | bytes 1179656 | tf_op jit(solution)/shard_map/ppermute | solution.py:28
  267.3 3.7 collective-permute-start.14
  271.6 5.3 collective-permute-start.15
  273.7 10.0 %collective-permute-start.10 = (f32[8,16,16]{2,1,0:T(8,128)}, f32[8,16,16]{2,1,0:T(8,128)S(1)}, u32[]{:S(2)}, u32[]{:S(2)}) collective-permute-start(f32[8,16,16]{2,1,0:T(8,128)} %get-tuple-element.47), channel_id=1, source_target_pairs={{4,0},{8,4},{12,8},{16,12},{20,16},{24,20},{28,24},{0,28},{5,1},{9... | collective-permute-start | bytes 24584 | tf_op jit(solution)/shard_map/ppermute | solution.py:28
  276.1 7.7 %collective-permute-start.9 = (f32[8,16,16]{2,1,0:T(8,128)}, f32[8,16,16]{2,1,0:T(8,128)S(1)}, u32[]{:S(2)}, u32[]{:S(2)}) collective-permute-start(f32[8,16,16]{2,1,0:T(8,128)} %get-tuple-element.46), channel_id=1, source_target_pairs={{28,0},{0,4},{4,8},{8,12},{12,16},{16,20},{20,24},{24,28},{29,1},{... | collective-permute-start | bytes 24584 | tf_op jit(solution)/shard_map/ppermute | solution.py:28
  277.6 4.8 collective-permute-start.16
  277.6 6.8 %collective-permute-start.8 = (bf16[16,1536]{1,0:T(8,128)(2,1)S(1)}, bf16[16,1536]{1,0:T(8,128)(2,1)S(1)}, u32[]{:S(2)}, u32[]{:S(2)}) collective-permute-start(bf16[16,1536]{1,0:T(8,128)(2,1)S(1)} %get-tuple-element.49), channel_id=1, source_target_pairs={{4,0},{8,4},{12,8},{16,12},{20,16},{24,20},{28,24},{0,28},{5,1},{9... | collective-permute-start | bytes 147464 | tf_op jit(solution)/shard_map/ppermute | solution.py:28
  282.4 6.8 %collective-permute-start.7 = (bf16[16,1536]{1,0:T(8,128)(2,1)S(1)}, bf16[16,1536]{1,0:T(8,128)(2,1)S(1)}, u32[]{:S(2)}, u32[]{:S(2)}) collective-permute-start(bf16[16,1536]{1,0:T(8,128)(2,1)S(1)} %get-tuple-element.48), channel_id=1, source_target_pairs={{28,0},{0,4},{4,8},{8,12},{12,16},{16,20},{20,24},{24,28},{29,1},{... | collective-permute-start | bytes 147464 | tf_op jit(solution)/shard_map/ppermute | solution.py:28
  291.9 2.1 copy-start.7
  292.4 66.4 %copy-start.10 = (f32[2,768,128]{2,1,0:T(8,128)}, f32[2,768,128]{2,1,0:T(8,128)S(1)}, u32[]{:S(2)}) copy-start(f32[2,768,128]{2,1,0:T(8,128)S(1)} %get-tuple-element.12) | copy-start | bytes 2359300
  294.4 67.3 %slice-start = ((s8[18874368]{0:T(1024)(128)(4,1)}), s8[4194304]{0:T(1024)(128)(4,1)S(1)}, s32[]{:S(2)}) async-start(s8[18874368]{0:T(1024)(128)(4,1)} %bitcast.144), calls=%async_computation | async-start | bytes 8388608
  294.4 67.3 %slice-start.1 = ((s8[18874368]{0:T(1024)(128)(4,1)}), s8[4194304]{0:T(1024)(128)(4,1)S(1)}, s32[]{:S(2)}) async-start(s8[18874368]{0:T(1024)(128)(4,1)} %bitcast.144), calls=%async_computation.1 | async-start | bytes 8388608
  327.3 34.3 %slice-start.2 = ((s8[18874368]{0:T(1024)(128)(4,1)}), s8[4194304]{0:T(1024)(128)(4,1)S(1)}, s32[]{:S(2)}) async-start(s8[18874368]{0:T(1024)(128)(4,1)} %bitcast.144), calls=%async_computation.2 | async-start | bytes 8388608
  327.4 14.1 %collective-permute-start.17 = (f32[768,128]{1,0:T(8,128)S(1)}, f32[768,128]{1,0:T(8,128)S(1)}, u32[]{:S(2)}, u32[]{:S(2)}) collective-permute-start(f32[768,128]{1,0:T(8,128)S(1)} %get-tuple-element.28), channel_id=1, source_target_pairs={{4,0},{8,4},{12,8},{16,12},{20,16},{24,20},{28,24},{0,28},{5,1},{9... | collective-permute-start | bytes 1179656 | tf_op jit(solution)/shard_map/ppermute | solution.py:28
  327.5 14.4 %collective-permute-start.18 = (f32[768,128]{1,0:T(8,128)S(1)}, f32[768,128]{1,0:T(8,128)S(1)}, u32[]{:S(2)}, u32[]{:S(2)}) collective-permute-start(f32[768,128]{1,0:T(8,128)S(1)} %get-tuple-element.27), channel_id=1, source_target_pairs={{28,0},{0,4},{4,8},{8,12},{12,16},{16,20},{20,24},{24,28},{29,1},{... | collective-permute-start | bytes 1179656 | tf_op jit(solution)/shard_map/ppermute | solution.py:28
  343.1 3.7 collective-permute-start.19
  346.8 3.9 collective-permute-start.20
  350.7 4.8 collective-permute-start.21
  356.8 4.8 slice-start.3
  358.8 2.8 slice-start.4
  394.6 17.8 %copy-start.3 = (f32[2,1536,128]{2,1,0:T(8,128)S(1)}, f32[2,1536,128]{2,1,0:T(8,128)}, u32[]{:S(2)}) copy-start(f32[2,1536,128]{2,1,0:T(8,128)} %fusion.20) | copy-start | bytes 4718596
  396.1 16.3 %collective-permute-start.22 = (f32[768,128]{1,0:T(8,128)S(1)}, f32[768,128]{1,0:T(8,128)S(1)}, u32[]{:S(2)}, u32[]{:S(2)}) collective-permute-start(f32[768,128]{1,0:T(8,128)S(1)} %get-tuple-element.25), channel_id=1, source_target_pairs={{4,0},{8,4},{12,8},{16,12},{20,16},{24,20},{28,24},{0,28},{5,1},{9... | collective-permute-start | bytes 1179656 | tf_op jit(solution)/shard_map/ppermute | solution.py:28
  401.3 11.5 %collective-permute-start.23 = (f32[768,128]{1,0:T(8,128)S(1)}, f32[768,128]{1,0:T(8,128)S(1)}, u32[]{:S(2)}, u32[]{:S(2)}) collective-permute-start(f32[768,128]{1,0:T(8,128)S(1)} %get-tuple-element.24), channel_id=1, source_target_pairs={{28,0},{0,4},{4,8},{8,12},{12,16},{16,20},{20,24},{24,28},{29,1},{... | collective-permute-start | bytes 1179656 | tf_op jit(solution)/shard_map/ppermute | solution.py:28
  413.1 14.4 %copy-start.13 = (f32[2,768,128]{2,1,0:T(8,128)}, f32[2,768,128]{2,1,0:T(8,128)S(1)}, u32[]{:S(2)}) copy-start(f32[2,768,128]{2,1,0:T(8,128)S(1)} %maximum_negate_fusion.4) | copy-start | bytes 2359300
  414.0 3.7 collective-permute-start.24
  417.7 3.7 collective-permute-start.25
  421.5 4.8 collective-permute-start.26
  464.9 11.4 %collective-permute-start.27 = (f32[768,128]{1,0:T(8,128)S(1)}, f32[768,128]{1,0:T(8,128)S(1)}, u32[]{:S(2)}, u32[]{:S(2)}) collective-permute-start(f32[768,128]{1,0:T(8,128)S(1)} %get-tuple-element.22), channel_id=1, source_target_pairs={{4,0},{8,4},{12,8},{16,12},{20,16},{24,20},{28,24},{0,28},{5,1},{9... | collective-permute-start | bytes 1179656 | tf_op jit(solution)/shard_map/ppermute | solution.py:28
  471.0 10.6 %collective-permute-start.28 = (f32[768,128]{1,0:T(8,128)S(1)}, f32[768,128]{1,0:T(8,128)S(1)}, u32[]{:S(2)}, u32[]{:S(2)}) collective-permute-start(f32[768,128]{1,0:T(8,128)S(1)} %get-tuple-element.21), channel_id=1, source_target_pairs={{28,0},{0,4},{4,8},{8,12},{12,16},{16,20},{20,24},{24,28},{29,1},{... | collective-permute-start | bytes 1179656 | tf_op jit(solution)/shard_map/ppermute | solution.py:28
  482.8 3.7 collective-permute-start.29
  486.5 3.7 collective-permute-start.30
  490.2 4.8 collective-permute-start.31
  (14 other events, 16.6 us)
